TPU v7x, 32 devices: a whole 2x2x4 slice. The times are simulated.
32 devices in a mesh: seq: 8 (over y, x, core), head: 4 (over z).
Axes of the slice: x: 2, y: 2, z: 4, core: 2. Of those that a mesh axis runs over, the one named last changes fastest.
Arguments:
- q2: bfloat16 [2048, 4096], P('seq', 'head'), may hold values from -128 to 128
- k2: bfloat16 [2048, 512], P('seq', 'head'), may hold values from -6 to 6
- v2: bfloat16 [2048, 512], P('seq', 'head'), may hold values from -6 to 6
- hidden: bfloat16 [2048, 8192], P('seq', 'head'), may hold values from -120 to 120
- w_query: bfloat16 [8192, 4096], P(None, 'head'), may hold values from -0.0625 to 0.0625
- b_query: float32 [4096], P('head'), may hold values from -3 to 3
- w_key: bfloat16 [8192, 512], P(None, 'head'), may hold values from -0.0625 to 0.0625
- b_key: float32 [512], P('head'), may hold values from -3 to 3
- w_value: bfloat16 [8192, 512], P(None, 'head'), may hold values from -0.0625 to 0.0625
- b_value: float32 [512], P('head'), may hold values from -3 to 3
- kept_index: int32 [2048], P('seq'), may hold values from 0 to 127, as said below
- block_count: int32 [16], P('seq'), may hold values from 0 to 128, as said below
- text_rows: int32 [256], replicated, may hold values from 0 to 2047, as said below
Outputs:
- attn2: bfloat16 [2048, 4096], P('seq', 'head')
- importance: float32 [2048], P('seq')
- attn3: bfloat16 [1152, 4096], P('seq', 'head')
Inputs may be any that keep to these rules, and one draw needn't show every extreme that they name: `kept_index`: in each aligned block of 128 rows, the first block_count entries are the in-block indices of that block's kept rows in ascending order; the other entries are the block's remaining indices. `block_count`: every text row is kept, and exactly 1152 rows are kept in all. For every k, the rows 2 * k * 256 to (2 * k + 2) * 256 - 1 hold exactly 288 kept rows together. `text_rows`: Distinct, in ascending order.
All inputs are finite; a program needn't handle non-finite values.
Results may differ from a plain program's by a relative error of at most 0.0093.
Values may be sent and summed in bfloat16 or wider, within the bound.
A program may use at most 128 MiB of HBM per device.

v0:
```python
import math

import jax
import jax.numpy as jnp
from jax import lax
from jax.sharding import PartitionSpec as P

HD = 128
GROUP = 8
BLOCK = 128
TEXT = 256


def carried_in(part, axis, combine, identity):
    place = lax.axis_index(axis)
    gathered = lax.all_gather(part, axis)
    state = jnp.zeros_like(part) + jnp.asarray(identity, part.dtype)

    def one(turn, state):
        return combine(state, lax.dynamic_index_in_dim(gathered, turn, 0, False))

    return lax.fori_loop(0, place, one, state)


def shifted(block, axis, distance):
    devices = range(lax.axis_size(axis))
    route = [(i - distance, i) for i in devices if i - distance in devices]
    return lax.ppermute(block, axis, route)


def rotate(values, positions):
    half = values.shape[-1] // 2
    freqs = 1000000.0 ** (-(jnp.arange(half, dtype=jnp.float32) * 2.0) / values.shape[-1])
    angles = positions.astype(jnp.float32)[:, None] * freqs[None, :]
    cosine = jnp.cos(angles)[:, None, :]
    sine = jnp.sin(angles)[:, None, :]
    first = values[..., :half]
    second = values[..., half:]
    return jnp.concatenate(
        [first * cosine - second * sine, second * cosine + first * sine], axis=-1
    )


def start_carry(count):
    return (
        jnp.full((GROUP, count), -1e30, jnp.float32),
        jnp.zeros((GROUP, count), jnp.float32),
        jnp.zeros((count, GROUP, HD), jnp.float32),
    )


def finish(carry):
    _, total, summed = carry
    return (summed / total.T[:, :, None]).reshape(summed.shape[0], -1).astype(jnp.bfloat16)


def attend(carry, queries, keys, values, query_pos, key_pos, key_live):
    count = keys.shape[0]
    width = 512 if count % 512 == 0 else count
    scale = 1.0 / math.sqrt(HD)

    def step(state, block):
        top, total, summed = state
        key_block, value_block, place_block, live_block = block
        scores = (
            jnp.einsum("qgd,kd->gqk", queries, key_block, preferred_element_type=jnp.float32)
            * scale
        )
        allowed = ((place_block[None, :] <= query_pos[:, None]) & live_block[None, :])[None]
        new_top = jnp.maximum(top, jnp.max(jnp.where(allowed, scores, -1e30), axis=-1))
        rescale = jnp.exp(top - new_top)
        weights = jnp.where(allowed, jnp.exp(scores - new_top[..., None]), 0.0)
        total = total * rescale + jnp.sum(weights, axis=-1)
        summed = summed * rescale.T[:, :, None] + jnp.einsum(
            "gqk,kd->qgd",
            weights.astype(jnp.bfloat16),
            value_block,
            preferred_element_type=jnp.float32,
        )
        return ((new_top, total, summed), None)

    blocks = count // width
    pieces = (
        keys.reshape(blocks, width, -1),
        values.reshape(blocks, width, -1),
        key_pos.reshape(blocks, width),
        key_live.reshape(blocks, width),
    )
    carry, _ = lax.scan(step, carry, pieces)
    return carry


def project(inputs, positions, w_query, b_query, w_key, b_key, w_value, b_value):
    count = inputs.shape[0]
    query_part = jnp.dot(inputs, w_query, preferred_element_type=jnp.float32) + b_query
    query_part = rotate(query_part.reshape(count, -1, HD), positions).astype(jnp.bfloat16)
    key_part = jnp.dot(inputs, w_key, preferred_element_type=jnp.float32) + b_key
    key_part = (
        rotate(key_part.reshape(count, 1, HD), positions).reshape(count, HD).astype(jnp.bfloat16)
    )
    value_part = (jnp.dot(inputs, w_value, preferred_element_type=jnp.float32) + b_value).astype(
        jnp.bfloat16
    )
    return (query_part, key_part, value_part)


def pick_rows(table, valid, source):
    return jnp.where(valid[:, None], jnp.take(table, source, axis=0), jnp.zeros((), table.dtype))


def body(
    q2,
    k2,
    v2,
    hidden,
    w_query,
    b_query,
    w_key,
    b_key,
    w_value,
    b_value,
    kept_index,
    block_count,
    text_rows,
):
    rows = q2.shape[0]
    seq_count = lax.axis_size("seq")
    head_count = lax.axis_size("head")
    seq_rank = lax.axis_index("seq")
    first_row = seq_rank * rows
    query_pos = first_row + jnp.arange(rows, dtype=jnp.int32)
    queries = q2.reshape(rows, GROUP, HD)
    keys = lax.all_gather(k2, "seq", axis=0, tiled=True)
    values = lax.all_gather(v2, "seq", axis=0, tiled=True)
    key_pos = jnp.arange(keys.shape[0], dtype=jnp.int32)
    carry = attend(
        start_carry(rows),
        queries,
        keys,
        values,
        query_pos,
        key_pos,
        jnp.ones((keys.shape[0],), jnp.bool_),
    )
    top, total, _ = carry
    attn2 = finish(carry)
    selector = text_rows[:, None] == query_pos[None, :]
    picked = jnp.dot(selector.astype(jnp.bfloat16), q2, preferred_element_type=jnp.float32)
    picked_top = jnp.dot(selector.astype(jnp.float32), top.T, precision=lax.Precision.HIGHEST)
    picked_total = jnp.dot(selector.astype(jnp.float32), total.T, precision=lax.Precision.HIGHEST)
    text_queries, text_top, text_total = (
        lax.psum(picked.astype(jnp.bfloat16), "seq").astype(jnp.float32),
        lax.psum(picked_top.astype(jnp.bfloat16), "seq").astype(jnp.float32),
        lax.psum(picked_total.astype(jnp.bfloat16), "seq").astype(jnp.float32),
    )
    text_block = text_queries.astype(jnp.bfloat16).reshape(TEXT, GROUP, HD)
    scores = jnp.einsum("tgd,kd->gtk", text_block, k2, preferred_element_type=jnp.float32) * (
        1.0 / math.sqrt(HD)
    )
    allowed = (query_pos[None, :] <= text_rows[:, None])[None]
    probs = jnp.where(
        allowed, jnp.exp(scores - text_top.T[:, :, None]) / text_total.T[:, :, None], 0.0
    )
    partial_value = jnp.sum(probs, axis=(0, 1))
    head_total = lax.psum(partial_value, "head")
    importance = head_total * (rows * seq_count / (GROUP * head_count * TEXT))
    blocks = rows // BLOCK
    kept_count = jnp.sum(block_count)
    ends = jnp.cumsum(block_count)
    begins = ends - block_count
    ranks = jnp.arange(rows, dtype=jnp.int32)
    owner = jnp.minimum(
        jnp.sum((ranks[:, None] >= ends[None, :]).astype(jnp.int32), axis=1), blocks - 1
    )
    within = jnp.clip(ranks - begins[owner], 0, BLOCK - 1)
    compact = owner * BLOCK + kept_index[owner * BLOCK + within]
    per_device = (rows * seq_count + TEXT) // (2 * seq_count)
    offset = carried_in(kept_count, "seq", lambda earlier, later: earlier + later, jnp.int32(0))

    def window(delta):
        place = (seq_rank + delta) * per_device + jnp.arange(per_device, dtype=jnp.int32) - offset
        near_valid = (place >= 0) & (place < kept_count)
        return (near_valid, compact[jnp.clip(place, 0, rows - 1)])

    own_valid, own_source = window(0)
    gathered = pick_rows(hidden, own_valid, own_source).astype(jnp.float32)
    kept_pos = jnp.where(own_valid, first_row + own_source, 0)
    for delta in (1, -1):
        near_valid, near_source = window(delta)
        sent = pick_rows(hidden, near_valid, near_source)
        gathered = gathered + shifted(sent, "seq", delta).astype(jnp.float32)
        near_places = jnp.where(near_valid, first_row + near_source, 0)
        kept_pos = kept_pos + shifted(near_places, "seq", delta)
    kept_rows = gathered.astype(jnp.bfloat16)
    full_rows = lax.all_gather(kept_rows, "head", axis=1, tiled=True)
    queries3, keys3, values3 = project(
        full_rows, kept_pos, w_query, b_query, w_key, b_key, w_value, b_value
    )
    order_pos = seq_rank * per_device + jnp.arange(per_device, dtype=jnp.int32)
    keys = lax.all_gather(keys3, "seq", axis=0, tiled=True)
    values = lax.all_gather(values3, "seq", axis=0, tiled=True)
    key_pos = jnp.arange(keys.shape[0], dtype=jnp.int32)
    state = attend(
        start_carry(per_device),
        queries3,
        keys,
        values,
        order_pos,
        key_pos,
        jnp.ones((keys.shape[0],), jnp.bool_),
    )
    attn3 = finish(state)
    return (attn2, importance, attn3)


def solution(mesh):
    placed = (
        P("seq", "head"),
        P("seq", "head"),
        P("seq", "head"),
        P("seq", "head"),
        P(None, "head"),
        P("head"),
        P(None, "head"),
        P("head"),
        P(None, "head"),
        P("head"),
        P("seq"),
        P("seq"),
        P(),
    )
    return jax.shard_map(
        body,
        mesh=mesh,
        in_specs=placed,
        out_specs=(P("seq", "head"), P("seq"), P("seq", "head")),
        check_vma=False,
    )
```

profile of v0, /device:TPU:0, one launch (start us, length us, event | category | flops | bytes accessed | tf_op | source)
XLA Modules:
  0.0 204.4 jit_solution(179218920697752603)
XLA Ops:
  8.1 1.0 reduce-window.8
  9.1 1.3 fusion.90
  10.4 1.2 dynamic-slice.2
  11.6 1.4 dynamic-update-slice
  13.0 9.5 %all-reduce = s32[8]{0:T(128)S(1)} all-reduce(s32[8]{0:T(128)S(1)} %dynamic-update-slice), channel_id=1, replica_groups=mesh['seq'=8,'head'=4] {'seq'}, use_global_device_ids=true, to_apply=%add | all-reduce | flops 8 | bytes 64
  22.5 0.6 fusion.91
  23.2 1.3 compare_select_fusion.3
  24.5 2.0 gather_fusion
  26.5 1.6 gather_fusion.2
  28.2 0.6 add_select_fusion.1
  28.8 1.5 collective-permute-start.2
  30.3 1.6 gather_fusion.3
  31.9 0.6 add_select_fusion
  32.6 1.3 collective-permute-start.3
  33.9 1.8 gather_fusion.5
  35.7 2.1 %select_select_fusion.1 = bf16[144,2048]{1,0:T(8,128)(2,1)} fusion(bf16[144,2048]{1,0:T(8,128)(2,1)} %gather_fusion.5, pred[144]{0:T(512)(128)(4,1)S(1)} %compare_and_fusion.1, pred[144]{0:T(512)(128)(4,1)S(1)} %get-tuple-element.191), kind=kLoop, calls=%fused_computation.75 | loop fusion | flops 589824 | bytes 1179936 | tf_op jit(solution)/shard_map/jit(_where)/select_n | solution.py:108
  37.8 7.3 %collective-permute-start = (bf16[144,2048]{1,0:T(8,128)(2,1)}, bf16[144,2048]{1,0:T(8,128)(2,1)}, u32[]{:S(2)}, u32[]{:S(2)}) collective-permute-start(bf16[144,2048]{1,0:T(8,128)(2,1)} %select_select_fusion.1), channel_id=1, source_target_pairs={{0,4},{4,8},{8,12},{12,16},{16,20},{20,24},{24,28},{1,5},{5,9},{9,... | collective-permute-start | bytes 1769480 | tf_op jit(solution)/shard_map/ppermute | solution.py:28
  45.1 1.8 gather_fusion.6
  47.0 2.1 %select_select_fusion = bf16[144,2048]{1,0:T(8,128)(2,1)} fusion(bf16[144,2048]{1,0:T(8,128)(2,1)} %gather_fusion.6, pred[144]{0:T(512)(128)(4,1)S(1)} %compare_and_fusion, pred[144]{0:T(512)(128)(4,1)S(1)} %get-tuple-element.193), kind=kLoop, calls=%fused_computation.74 | loop fusion | flops 589824 | bytes 1179936 | tf_op jit(solution)/shard_map/jit(_where)/select_n | solution.py:108
  49.1 1.3 collective-permute-start.1
  50.4 1.4 fusion.44
  51.8 0.9 copy.53
  52.8 1.6 gather_fusion.1
  54.5 17.4 %all_gather.21 = bf16[2048,128]{1,0:T(8,128)(2,1)} all-gather(bf16[256,128]{1,0:T(8,128)(2,1)S(1)} %copy-done.6), channel_id=1, replica_groups=mesh['seq'=8,'head'=4] {'seq'}, dimensions={0}, use_global_device_ids=true | all-gather | bytes 589824 | tf_op jit(solution)/shard_map/all_gather | solution.py:133
  71.9 10.2 %all_gather.22 = bf16[2048,128]{1,0:T(8,128)(2,1)} all-gather(bf16[256,128]{1,0:T(8,128)(2,1)S(1)} %copy-done.5), channel_id=1, replica_groups=mesh['seq'=8,'head'=4] {'seq'}, dimensions={0}, use_global_device_ids=true | all-gather | bytes 589824 | tf_op jit(solution)/shard_map/all_gather | solution.py:134
  82.1 2.0 copy.31
  84.1 2.1 %copy.32 = bf16[256,8,128]{2,0,1:T(8,128)(2,1)} copy(bf16[256,8,128]{0,2,1:T(8,128)(2,1)} %bitcast.171) | data formatting | bytes 1048576
  86.2 0.6 add_convert_fusion.2
  86.9 1.8 gather_fusion.4
  88.7 2.7 %add_convert_fusion = bf16[144,2048]{1,0:T(8,128)(2,1)} fusion(bf16[144,2048]{1,0:T(8,128)(2,1)} %collective-permute-done.1, bf16[144,2048]{1,0:T(8,128)(2,1)} %collective-permute-done, bf16[144,2048]{1,0:T(8,128)(2,1)} %gather_fusion.4, pred[144]{0:T(512)(128)(4,1)S(1)} %compare_and_fusion.2, pred[144]{0:T(512)(128)(4,1)S(1)} %get-tuple-element.189), kind=kLoop, calls=%fused_computation.60 | loop fusion | flops 2359296 | bytes 2359584 | tf_op jit(solution)/shard_map/convert_element_type | solution.py:194
  91.5 38.3 %while.32 = (s32[]{:T(128)}, f32[8,256]{1,0:T(8,128)S(1)}, f32[8,256]{1,0:T(8,128)S(1)}, f32[256,8,128]{0,2,1:T(8,128)}, s32[4,512]{1,0:T(4,128)S(1)}, /*index=5...) while((s32[]{:T(128)}, f32[8,256]{1,0:T(8,128)S(1)}, ...), condition=%wide.region_3.4_spmd.clone, body=%wide.region_0.3_spmd.clone.sunk | while | flops 549335296 | bytes 32908444 | solution.py:89
  91.7 3.8 %fusion.114 = (f32[8,256]{1,0:T(8,128)S(1)}, f32[512,256,8]{1,0,2:T(8,128)}) fusion(pred[256,512]{0,1:T(8,128)(4,1)S(1)} %broadcast_compare_fusion.3, bf16[256,8,128]{2,0,1:T(8,128)(2,1)} %get-tuple-element.332, bf16[4,512,128]{2,1,0:T(8,128)(2,1)} %get-tuple-element.331, s32[]{:T(128)} %get-tuple-element.315), kind=kOutput, calls=%fused_computation.10.clone.1 | convolution fusion | flops 271579136 | bytes 4989440 | tf_op jit(solution)/shard_map/while/body/eval_jaxpr/qgd,kd->gqk/dot_general | solution.py:66
  95.5 4.4 %fusion.118 = f32[256,8,128]{0,2,1:T(8,128)} fusion(f32[512,256,8]{1,0,2:T(8,128)} %get-tuple-element.302, f32[8,256]{1,0:T(8,128)S(1)} %get-tuple-element.327, pred[256,512]{0,1:T(8,128)(4,1)S(1)} %broadcast_compare_fusion.3, f32[256,8,128]{0,2,1:T(8,128)} %get-tuple-element.318, f32[256,8]{0,1:T(8,128)S(1)} %get-tuple-element.303, ...), kind=kOutput, calls=%fused_computation.18.clone.1 | convolution fusion | flops 273416192 | bytes 6570497 | tf_op jit(solution)/shard_map/while/body/eval_jaxpr/gqk,kd->qgd/dot_general | solution.py:74
  99.9 0.9 fusion.116
  101.0 3.8 %fusion.114 = (f32[8,256]{1,0:T(8,128)S(1)}, f32[512,256,8]{1,0,2:T(8,128)}) fusion(pred[256,512]{0,1:T(8,128)(4,1)S(1)} %broadcast_compare_fusion.3, bf16[256,8,128]{2,0,1:T(8,128)(2,1)} %get-tuple-element.332, bf16[4,512,128]{2,1,0:T(8,128)(2,1)} %get-tuple-element.331, s32[]{:T(128)} %get-tuple-element.315), kind=kOutput, calls=%fused_computation.10.clone.1 | convolution fusion | flops 271579136 | bytes 4989440 | tf_op jit(solution)/shard_map/while/body/eval_jaxpr/qgd,kd->gqk/dot_general | solution.py:66
  104.8 4.7 %fusion.118 = f32[256,8,128]{0,2,1:T(8,128)} fusion(f32[512,256,8]{1,0,2:T(8,128)} %get-tuple-element.302, f32[8,256]{1,0:T(8,128)S(1)} %get-tuple-element.327, pred[256,512]{0,1:T(8,128)(4,1)S(1)} %broadcast_compare_fusion.3, f32[256,8,128]{0,2,1:T(8,128)} %get-tuple-element.318, f32[256,8]{0,1:T(8,128)S(1)} %get-tuple-element.303, ...), kind=kOutput, calls=%fused_computation.18.clone.1 | convolution fusion | flops 273416192 | bytes 6570497 | tf_op jit(solution)/shard_map/while/body/eval_jaxpr/gqk,kd->qgd/dot_general | solution.py:74
  109.5 0.9 fusion.116
  110.6 3.8 %fusion.114 = (f32[8,256]{1,0:T(8,128)S(1)}, f32[512,256,8]{1,0,2:T(8,128)}) fusion(pred[256,512]{0,1:T(8,128)(4,1)S(1)} %broadcast_compare_fusion.3, bf16[256,8,128]{2,0,1:T(8,128)(2,1)} %get-tuple-element.332, bf16[4,512,128]{2,1,0:T(8,128)(2,1)} %get-tuple-element.331, s32[]{:T(128)} %get-tuple-element.315), kind=kOutput, calls=%fused_computation.10.clone.1 | convolution fusion | flops 271579136 | bytes 4989440 | tf_op jit(solution)/shard_map/while/body/eval_jaxpr/qgd,kd->gqk/dot_general | solution.py:66
  114.5 4.7 %fusion.118 = f32[256,8,128]{0,2,1:T(8,128)} fusion(f32[512,256,8]{1,0,2:T(8,128)} %get-tuple-element.302, f32[8,256]{1,0:T(8,128)S(1)} %get-tuple-element.327, pred[256,512]{0,1:T(8,128)(4,1)S(1)} %broadcast_compare_fusion.3, f32[256,8,128]{0,2,1:T(8,128)} %get-tuple-element.318, f32[256,8]{0,1:T(8,128)S(1)} %get-tuple-element.303, ...), kind=kOutput, calls=%fused_computation.18.clone.1 | convolution fusion | flops 273416192 | bytes 6570497 | tf_op jit(solution)/shard_map/while/body/eval_jaxpr/gqk,kd->qgd/dot_general | solution.py:74
  119.2 0.9 fusion.116
  120.3 3.8 %fusion.114 = (f32[8,256]{1,0:T(8,128)S(1)}, f32[512,256,8]{1,0,2:T(8,128)}) fusion(pred[256,512]{0,1:T(8,128)(4,1)S(1)} %broadcast_compare_fusion.3, bf16[256,8,128]{2,0,1:T(8,128)(2,1)} %get-tuple-element.332, bf16[4,512,128]{2,1,0:T(8,128)(2,1)} %get-tuple-element.331, s32[]{:T(128)} %get-tuple-element.315), kind=kOutput, calls=%fused_computation.10.clone.1 | convolution fusion | flops 271579136 | bytes 4989440 | tf_op jit(solution)/shard_map/while/body/eval_jaxpr/qgd,kd->gqk/dot_general | solution.py:66
  124.1 4.7 %fusion.118 = f32[256,8,128]{0,2,1:T(8,128)} fusion(f32[512,256,8]{1,0,2:T(8,128)} %get-tuple-element.302, f32[8,256]{1,0:T(8,128)S(1)} %get-tuple-element.327, pred[256,512]{0,1:T(8,128)(4,1)S(1)} %broadcast_compare_fusion.3, f32[256,8,128]{0,2,1:T(8,128)} %get-tuple-element.318, f32[256,8]{0,1:T(8,128)S(1)} %get-tuple-element.303, ...), kind=kOutput, calls=%fused_computation.18.clone.1 | convolution fusion | flops 273416192 | bytes 6570497 | tf_op jit(solution)/shard_map/while/body/eval_jaxpr/gqk,kd->qgd/dot_general | solution.py:74
  128.8 0.9 fusion.116
  129.7 0.3 fusion.52
  130.0 0.3 fusion.51
  130.3 14.4 %all-reduce.1 = (bf16[8,256]{1,0:T(8,128)(2,1)S(1)}, bf16[8,256]{1,0:T(8,128)(2,1)S(1)}) all-reduce(bf16[8,256]{1,0:T(8,128)(2,1)S(1)} %fusion.52, bf16[8,256]{1,0:T(8,128)(2,1)S(1)} %fusion.51), channel_id=1, replica_groups=mesh['seq'=8,'head'=4] {'seq'}, use_global_device_ids=true, to_apply=%region_6.7 | all-reduce | flops 4096 | bytes 16384 | tf_op jit(solution)/shard_map/psum | solution.py:154
  144.7 1.3 divide_convert_fusion
  146.0 1.0 copy.40
  147.3 0.3 multiply_cosine_fusion
  147.7 1.8 fusion.40
  149.5 11.8 %psum.31 = f32[256]{0:T(256)S(1)} all-reduce(f32[256]{0:T(256)S(1)} %fusion.40), channel_id=1, replica_groups=mesh['seq'=8,'head'=4] {'head'}, use_global_device_ids=true, to_apply=%region_8.9 | all-reduce | flops 256 | bytes 2048 | tf_op jit(solution)/shard_map/psum | solution.py:165
  161.3 0.6 broadcast_multiply_fusion
  161.9 9.4 %fusion.48 = f32[18,8,8,128]{3,1,2,0:T(8,128)S(1)} fusion(bf16[144,8192]{1,0:T(8,128)(2,1)} %all-gather.3.cloned.1.call-done, bf16[8192,1024]{1,0:T(8,128)(2,1)} %param.23, f32[1024]{0:T(1024)S(1)} %copy-done.8), kind=kOutput, calls=%fused_computation.59 | convolution fusion | flops 2416066560 | bytes 19730432 | tf_op jit(solution)/shard_map/dot_general | solution.py:95
  171.6 0.8 fusion.49
  172.4 0.4 fusion.81
  172.9 9.1 %all-gather = bf16[1152,1,128]{2,0,1:T(8,128)(2,1)S(1)} all-gather(bf16[144,1,128]{2,0,1:T(8,128)(2,1)S(1)} %pad_maximum_fusion), channel_id=2, replica_groups=mesh['seq'=8,'head'=4] {'seq'}, dimensions={0}, use_global_device_ids=true | all-gather | bytes 331776 | tf_op jit(solution)/shard_map/all_gather | solution.py:200
  182.0 0.2 subtract_convert_fusion
  182.2 1.4 fusion.27
  183.7 1.3 fusion.30
  185.0 0.2 copy-done.4
  185.2 0.8 fusion.50
  186.0 8.8 %all_gather.27 = bf16[1152,128]{1,0:T(8,128)(2,1)S(1)} all-gather(bf16[144,128]{1,0:T(8,128)(2,1)S(1)} %fusion.50), channel_id=1, replica_groups=mesh['seq'=8,'head'=4] {'seq'}, dimensions={0}, use_global_device_ids=true | all-gather | bytes 331776 | tf_op jit(solution)/shard_map/all_gather | solution.py:201
  194.8 1.4 fusion.59
  196.2 0.8 copy.54
  (95 shorter events, 1.9 us)
Async XLA Ops:
  8.0 163.6 %copy-start = (bf16[8192,128]{1,0:T(8,128)(2,1)S(1)}, bf16[8192,128]{1,0:T(8,128)(2,1)}, u32[]{:S(2)}) copy-start(bf16[8192,128]{1,0:T(8,128)(2,1)} %param.25) | copy-start | bytes 6291460
  8.0 25.9 %copy-start.2 = (bf16[256,2048]{1,0:T(8,128)(2,1)S(1)}, bf16[256,2048]{1,0:T(8,128)(2,1)}, u32[]{:S(2)}) copy-start(bf16[256,2048]{1,0:T(8,128)(2,1)} %param.22) | copy-start | bytes 3145732
  8.0 139.7 %all-reduce.4.cloned.1.call-start = ((), (), s32[]{:S(2)}) async-start(), calls=%async_computation | async-start | bytes 1048576 | tf_op jit(solution)/shard_map/psum | solution.py:152
  28.8 57.4 %collective-permute-start.2 = (s32[144]{0:T(256)S(1)}, s32[144]{0:T(256)S(1)}, u32[]{:S(2)}, u32[]{:S(2)}) collective-permute-start(s32[144]{0:T(256)S(1)} %get-tuple-element.190), channel_id=1, source_target_pairs={{0,4},{4,8},{8,12},{12,16},{16,20},{20,24},{24,28},{1,5},{5,9},{9,... | collective-permute-start | bytes 1736 | tf_op jit(solution)/shard_map/ppermute | solution.py:28
  32.6 53.6 %collective-permute-start.3 = (s32[144]{0:T(256)S(1)}, s32[144]{0:T(256)S(1)}, u32[]{:S(2)}, u32[]{:S(2)}) collective-permute-start(s32[144]{0:T(256)S(1)} %get-tuple-element.192), channel_id=1, source_target_pairs={{4,0},{8,4},{12,8},{16,12},{20,16},{24,20},{28,24},{5,1},{9,5},{13... | collective-permute-start | bytes 1736 | tf_op jit(solution)/shard_map/ppermute | solution.py:28
  35.7 14.6 %copy-start.7 = (s32[256]{0:T(256)S(1)}, s32[256]{0:T(256)}, u32[]{:S(2)}) copy-start(s32[256]{0:T(256)} %param.31) | copy-start | bytes 3076
  37.8 50.9 %collective-permute-start = (bf16[144,2048]{1,0:T(8,128)(2,1)}, bf16[144,2048]{1,0:T(8,128)(2,1)}, u32[]{:S(2)}, u32[]{:S(2)}) collective-permute-start(bf16[144,2048]{1,0:T(8,128)(2,1)} %select_select_fusion.1), channel_id=1, source_target_pairs={{0,4},{4,8},{8,12},{12,16},{16,20},{20,24},{24,28},{1,5},{5,9},{9,... | collective-permute-start | bytes 1769480 | tf_op jit(solution)/shard_map/ppermute | solution.py:28
  45.1 9.3 %copy-start.6 = (bf16[256,128]{1,0:T(8,128)(2,1)S(1)}, bf16[256,128]{1,0:T(8,128)(2,1)}, u32[]{:S(2)}) copy-start(bf16[256,128]{1,0:T(8,128)(2,1)} %param.20) | copy-start | bytes 196612
  45.1 26.8 %copy-start.5 = (bf16[256,128]{1,0:T(8,128)(2,1)S(1)}, bf16[256,128]{1,0:T(8,128)(2,1)}, u32[]{:S(2)}) copy-start(bf16[256,128]{1,0:T(8,128)(2,1)} %param.21) | copy-start | bytes 196612
  49.1 39.6 %collective-permute-start.1 = (bf16[144,2048]{1,0:T(8,128)(2,1)}, bf16[144,2048]{1,0:T(8,128)(2,1)}, u32[]{:S(2)}, u32[]{:S(2)}) collective-permute-start(bf16[144,2048]{1,0:T(8,128)(2,1)} %select_select_fusion), channel_id=1, source_target_pairs={{4,0},{8,4},{12,8},{16,12},{20,16},{24,20},{28,24},{5,1},{9,5},{13... | collective-permute-start | bytes 1769480 | tf_op jit(solution)/shard_map/ppermute | solution.py:28
  52.7 109.1 %all-gather.3.cloned.1.call-start = ((), (), s32[]{:S(2)}) async-start(), calls=%async_computation.1 | async-start | bytes 2949120 | tf_op jit(solution)/shard_map/all_gather | solution.py:195
  95.5 4.4 %copy-start.1 = (f32[512,256,8]{1,0,2:T(8,128)S(1)}, f32[512,256,8]{1,0,2:T(8,128)}, u32[]{:S(2)}) copy-start(f32[512,256,8]{1,0,2:T(8,128)} %get-tuple-element.302) | copy-start | bytes 12582916 | tf_op jit(solution)/shard_map/while
  104.8 4.7 %copy-start.1 = (f32[512,256,8]{1,0,2:T(8,128)S(1)}, f32[512,256,8]{1,0,2:T(8,128)}, u32[]{:S(2)}) copy-start(f32[512,256,8]{1,0,2:T(8,128)} %get-tuple-element.302) | copy-start | bytes 12582916 | tf_op jit(solution)/shard_map/while
  114.5 4.7 %copy-start.1 = (f32[512,256,8]{1,0,2:T(8,128)S(1)}, f32[512,256,8]{1,0,2:T(8,128)}, u32[]{:S(2)}) copy-start(f32[512,256,8]{1,0,2:T(8,128)} %get-tuple-element.302) | copy-start | bytes 12582916 | tf_op jit(solution)/shard_map/while
  124.1 4.7 %copy-start.1 = (f32[512,256,8]{1,0,2:T(8,128)S(1)}, f32[512,256,8]{1,0,2:T(8,128)}, u32[]{:S(2)}) copy-start(f32[512,256,8]{1,0,2:T(8,128)} %get-tuple-element.302) | copy-start | bytes 12582916 | tf_op jit(solution)/shard_map/while
  147.7 14.2 %copy-start.8 = (f32[1024]{0:T(1024)S(1)}, f32[1024]{0:T(1024)}, u32[]{:S(2)}) copy-start(f32[1024]{0:T(1024)} %param.24) | copy-start | bytes 12292
  161.9 9.7 %copy-start.9 = (f32[128]{0:T(128)S(1)}, f32[128]{0:T(128)}, u32[]{:S(2)}) copy-start(f32[128]{0:T(128)} %param.26) | copy-start | bytes 1540
  161.9 9.7 %copy-start.3 = (bf16[144,8192]{1,0:T(8,128)(2,1)S(1)}, bf16[144,8192]{1,0:T(8,128)(2,1)}, u32[]{:S(2)}) copy-start(bf16[144,8192]{1,0:T(8,128)(2,1)} %all-gather.3.cloned.1.call-done) | copy-start | bytes 7077892
  183.6 1.6 copy-start.4
  183.6 1.6 copy-start.10
Sparse Core Ops, SparseCore 0:
  52.9 61.7 all-reduce.3
Sparse Core Ops, SparseCore 1:
  91.5 50.0 all-gather.2
where the time goes:
time: 205 us; the launch traced here: 204 us
  blocking collectives  81.1 us (40%)
  matrix products  51.4 us (25%)
  local copies, waits for them, and re-layouts  23 us (11%)
  other arithmetic  21.3 us (10%)
  between operations  15.9 us (8%)
  starting transfers between devices  11.4 us (6%)
    dot_general x5, matrix products, step(): jnp.einsum('gqk,kd->qgd', weights.astype(jnp.bfloat16), value_block, pref...  19.9 us
    all_gather x1, blocking collectives, body(): keys = lax.all_gather(k2, 'seq', axis=0, tiled=True)  17.4 us
    dot_general x5, matrix products, step(): jnp.einsum('qgd,kd->gqk', queries, key_block, preferred_element_type=jnp....  16.8 us
    psum x1, blocking collectives, body(): lax.psum(picked_total.astype(jnp.bfloat16), 'seq').astype(jnp.float32)  14.4 us
    psum x1, blocking collectives, body(): head_total = lax.psum(partial_value, 'head')  11.8 us
    ppermute x4, starting transfers between devices, shifted(): return lax.ppermute(block, axis, route)  11.3 us
    all_gather x1, blocking collectives, body(): values = lax.all_gather(v2, 'seq', axis=0, tiled=True)  10.2 us
    unnamed x1, blocking collectives  9.49 us
  transfers between devices with their start and end apart: 6, of which 0 were waited for; matrix products, arithmetic and copies ran while one was open for 33% of the time, Pallas kernels for 0%

commit v1 on v0

v1 whole, which is shorter than its diff:
```python
import functools
import math

import jax
import jax.numpy as jnp
from jax import lax
from jax.experimental import pallas as pl
from jax.experimental.pallas import tpu as pltpu
from jax.sharding import PartitionSpec as P

HD = 128
GROUP = 8
BLOCK = 128
THETA = 1000000.0


def chunk_width(count):
    width = 512
    while count % width:
        width -= 128
    return width


def loop(count, step, carry):
    if count <= 4:
        for turn in range(count):
            carry = step(turn, carry)
        return carry
    return lax.fori_loop(0, count, step, carry)


def attention_kernel(weigh, start_ref, q_ref, k_ref, v_ref, *rest):
    if weigh:
        text_ref, out_ref, imp_ref, score = rest
    else:
        out_ref, score = rest
    rows = q_ref.shape[0]
    count = k_ref.shape[0]
    width = score.shape[2]
    chunks = count // width
    queries = q_ref[...]
    row = start_ref[0] + lax.broadcasted_iota(jnp.int32, (rows, width), 0)
    ahead = row - lax.broadcasted_iota(jnp.int32, (rows, width), 1)
    scale = 1.0 / math.sqrt(HD)

    def span(turn):
        return pl.ds(pl.multiple_of(turn * width, 128), width)

    def first(turn, top):
        scores = lax.dot_general(
            queries, k_ref[span(turn), :], (((1,), (1,)), ((), ())), preferred_element_type=jnp.float32
        )
        scores = jnp.where(ahead >= turn * width, scores, -1e30)
        score[turn] = scores
        for part in range(width // 128):
            top = jnp.maximum(top, scores[:, part * 128 : (part + 1) * 128])
        return top

    top = loop(chunks, first, jnp.full((rows, 128), -1e30, jnp.float32))
    top = jnp.max(top, axis=1, keepdims=True)

    def second(turn, state):
        total, summed = state
        weights = jnp.exp((score[turn] - top) * scale)
        if weigh:
            score[turn] = weights
        for part in range(width // 128):
            total = total + weights[:, part * 128 : (part + 1) * 128]
        summed = summed + jnp.dot(
            weights.astype(jnp.bfloat16), v_ref[span(turn), :], preferred_element_type=jnp.float32
        )
        return (total, summed)

    blank = jnp.zeros((rows, 128), jnp.float32)
    total, summed = loop(chunks, second, (blank, blank))
    inverse = 1.0 / jnp.sum(total, axis=1, keepdims=True)
    out_ref[...] = (summed * inverse).astype(jnp.bfloat16)
    if weigh:

        @pl.when(pl.program_id(0) == 0)
        def _():
            imp_ref[...] = jnp.zeros_like(imp_ref)

        share = inverse * text_ref[...]

        def third(turn, state):
            part = jnp.sum(score[turn] * share, axis=0, keepdims=True)
            imp_ref[:, span(turn)] += part
            return state

        loop(chunks, third, 0)


def attention(start, queries, keys, values, text=None):
    rows, columns = queries.shape
    heads = columns // HD
    count = keys.shape[0]
    width = chunk_width(count)
    weigh = text is not None
    head_spec = pl.BlockSpec((rows, HD), lambda h, s: (0, h))
    whole = lambda shape: pl.BlockSpec(shape, lambda h, s: (0, 0))
    in_specs = [head_spec, whole((count, HD)), whole((count, HD))]
    operands = [queries, keys, values]
    out_shape = [jax.ShapeDtypeStruct((rows, columns), jnp.bfloat16)]
    out_specs = [head_spec]
    if weigh:
        in_specs.append(whole((rows, 1)))
        operands.append(text)
        out_shape.append(jax.ShapeDtypeStruct((1, count), jnp.float32))
        out_specs.append(whole((1, count)))
    return pl.pallas_call(
        functools.partial(attention_kernel, weigh),
        grid_spec=pltpu.PrefetchScalarGridSpec(
            num_scalar_prefetch=1,
            grid=(heads,),
            in_specs=in_specs,
            out_specs=out_specs,
            scratch_shapes=[pltpu.VMEM((count // width, rows, width), jnp.float32)],
        ),
        out_shape=out_shape,
        compiler_params=pltpu.CompilerParams(vmem_limit_bytes=40 * 1024 * 1024),
        cost_estimate=pl.CostEstimate(
            flops=4 * rows * columns * count, bytes_accessed=4 * rows * columns, transcendentals=rows * heads * count
        ),
    )(start.reshape(1), *operands)


def project_kernel(
    x_ref, wq_ref, wk_ref, wv_ref, bias_ref, cos_ref, sin_ref, q_ref, kv_ref, acc_q, acc_k, acc_v
):
    @pl.when(pl.program_id(0) == 0)
    def _():
        columns = acc_q.shape[1]
        acc_q[...] = jnp.broadcast_to(bias_ref[:, :columns], acc_q.shape)
        acc_k[...] = jnp.broadcast_to(bias_ref[:, columns : columns + HD], acc_k.shape)
        acc_v[...] = jnp.broadcast_to(bias_ref[:, columns + HD :], acc_v.shape)

    x = x_ref[...]
    acc_q[...] += jnp.dot(x, wq_ref[...], preferred_element_type=jnp.float32)
    acc_k[...] += jnp.dot(x, wk_ref[...], preferred_element_type=jnp.float32)
    acc_v[...] += jnp.dot(x, wv_ref[...], preferred_element_type=jnp.float32)

    @pl.when(pl.program_id(0) == pl.num_programs(0) - 1)
    def _():
        cosine, sine = cos_ref[...], sin_ref[...]

        def turned(u):
            return (u * cosine + pltpu.roll(u, HD // 2, 1) * sine).astype(jnp.bfloat16)

        for head in range(acc_q.shape[1] // HD):
            part = slice(head * HD, (head + 1) * HD)
            q_ref[:, part] = turned(acc_q[:, part])
        kv_ref[:, :HD] = turned(acc_k[...])
        kv_ref[:, HD:] = acc_v[...].astype(jnp.bfloat16)


def project(x, cosine, sine, w_query, w_key, w_value, bias):
    rows, depth = x.shape
    columns = w_query.shape[1]
    step = 1024
    whole = lambda shape: pl.BlockSpec(shape, lambda i: (0, 0))
    down = lambda width: pl.BlockSpec((step, width), lambda i: (i, 0))
    return pl.pallas_call(
        project_kernel,
        grid=(depth // step,),
        in_specs=[
            pl.BlockSpec((rows, step), lambda i: (0, i)),
            down(columns),
            down(HD),
            down(HD),
            whole((1, columns + 2 * HD)),
            whole((rows, HD)),
            whole((rows, HD)),
        ],
        out_specs=[whole((rows, columns)), whole((rows, 2 * HD))],
        out_shape=[
            jax.ShapeDtypeStruct((rows, columns), jnp.bfloat16),
            jax.ShapeDtypeStruct((rows, 2 * HD), jnp.bfloat16),
        ],
        scratch_shapes=[
            pltpu.VMEM((rows, columns), jnp.float32),
            pltpu.VMEM((rows, HD), jnp.float32),
            pltpu.VMEM((rows, HD), jnp.float32),
        ],
        compiler_params=pltpu.CompilerParams(vmem_limit_bytes=32 * 1024 * 1024),
        cost_estimate=pl.CostEstimate(
            flops=2 * rows * depth * (columns + 2 * HD),
            bytes_accessed=2 * depth * (columns + 2 * HD),
            transcendentals=0,
        ),
    )(x, w_query, w_key, w_value, bias, cosine, sine)


def body(
    q2, k2, v2, hidden, w_query, b_query, w_key, b_key, w_value, b_value, kept_index, block_count, text_rows
):
    rows = q2.shape[0]
    seq_count = lax.axis_size("seq")
    head_count = lax.axis_size("head")
    seq_rank = lax.axis_index("seq")
    first_row = seq_rank * rows
    text = text_rows.shape[0]
    per_device = (rows * seq_count + text) // (2 * seq_count)
    odd = seq_rank % 2

    blocks = rows // BLOCK
    ends = [block_count[0]]
    for b in range(1, blocks):
        ends.append(ends[-1] + block_count[b])
    kept_count = ends[-1]
    base = jnp.where(odd == 1, 2 * per_device - kept_count, 0)
    entry = jnp.arange(rows, dtype=jnp.int32)
    place = base + entry % BLOCK
    live = jnp.zeros((rows,), jnp.bool_)
    for b in range(blocks):
        inside = entry // BLOCK == b
        begin = ends[b] - block_count[b]
        place = place + jnp.where(inside, begin, 0)
        live = live | (inside & (entry % BLOCK < block_count[b]))
    source = (entry // BLOCK) * BLOCK + kept_index

    def window(start, count):
        order = start + jnp.arange(count, dtype=jnp.int32)
        hit = (order[:, None] == place[None, :]) & live[None, :]
        chosen = jnp.sum(jnp.where(hit, source[None, :] + 1, 0), axis=1) - 1
        select = (chosen[:, None] == jnp.arange(rows, dtype=jnp.int32)[None, :]).astype(jnp.bfloat16)
        picked = jnp.dot(select, hidden, preferred_element_type=jnp.float32).astype(jnp.bfloat16)
        return picked, jnp.where(chosen >= 0, chosen + first_row, 0)

    span = min(rows - per_device, per_device)
    swap = [(i, i + 1 - 2 * (i % 2)) for i in range(seq_count)]
    sent_rows, sent_pos = window(jnp.where(odd == 1, per_device - span, per_device), span)
    got_rows = lax.ppermute(sent_rows, "seq", swap)
    got_pos = lax.ppermute(sent_pos, "seq", swap)
    own_rows, own_pos = window(odd * per_device, per_device)
    rest = per_device - span
    low = jnp.where(odd == 1, 0, rest)

    def landed(got):
        shape = ((0, rest),) + ((0, 0),) * (got.ndim - 1)
        back = ((rest, 0),) + ((0, 0),) * (got.ndim - 1)
        return jnp.where(odd == 1, jnp.pad(got, shape), jnp.pad(got, back))

    kept_rows = own_rows + landed(got_rows)
    kept_pos = own_pos + landed(got_pos)
    full_rows = lax.all_gather(kept_rows, "head", axis=1, tiled=True)

    pairs = lax.all_gather(jnp.concatenate([k2, v2], axis=1), "seq", axis=0, tiled=True)
    query_pos = first_row + jnp.arange(rows, dtype=jnp.int32)
    is_text = jnp.any(query_pos[:, None] == text_rows[None, :], axis=1, keepdims=True).astype(jnp.float32)
    attn2, partial_value = attention(first_row, q2, pairs[:, :HD], pairs[:, HD:], is_text)
    head_total = lax.psum(partial_value.reshape(-1), ("seq", "head"))
    importance = lax.dynamic_slice_in_dim(head_total, first_row, rows, 0) * (
        rows * seq_count / (GROUP * head_count * text)
    )

    half = HD // 2
    freqs = THETA ** (-(jnp.arange(half, dtype=jnp.float32) * 2.0) / HD)
    angles = kept_pos.astype(jnp.float32)[:, None] * freqs[None, :]
    cosine, sine = jnp.cos(angles), jnp.sin(angles)
    cosine = jnp.concatenate([cosine, cosine], axis=1)
    sine = jnp.concatenate([-sine, sine], axis=1)
    bias = jnp.concatenate([b_query, b_key, b_value])[None, :]
    queries3, pair3 = project(full_rows, cosine, sine, w_query, w_key, w_value, bias)
    pairs3 = lax.all_gather(pair3, "seq", axis=0, tiled=True)
    (attn3,) = attention(seq_rank * per_device, queries3, pairs3[:, :HD], pairs3[:, HD:])
    return (attn2, importance, attn3)


def solution(mesh):
    placed = (
        P("seq", "head"),
        P("seq", "head"),
        P("seq", "head"),
        P("seq", "head"),
        P(None, "head"),
        P("head"),
        P(None, "head"),
        P("head"),
        P(None, "head"),
        P("head"),
        P("seq"),
        P("seq"),
        P(),
    )
    return jax.shard_map(
        body,
        mesh=mesh,
        in_specs=placed,
        out_specs=(P("seq", "head"), P("seq"), P("seq", "head")),
        check_vma=False,
    )
```

time: 205 us -> 132 us (0.64)
  matrix products: 51.4 us -> 1.52 us
  Pallas kernels: 0 us -> 28.5 us
  blocking collectives: 81.1 us -> 53.5 us
  waiting for transfers between devices: 0.07 us -> 18.7 us
  local copies, waits for them, and re-layouts: 23 us -> 7.11 us
  other arithmetic: 21.3 us -> 6.05 us
  starting transfers between devices: 11.4 us -> 0.72 us
    dot_general x17 -> x2, matrix products: 51.4 us -> 1.52 us  [window(): jnp.dot(select, hidden, preferred_element_type=jnp.float32)]
    all_gather x4 -> x1, blocking collectives: 45.5 us -> 10.8 us  [body(): pairs3 = lax.all_gather(pair3, 'seq', axis=0, tiled=True)]
    pallas_call x0 -> x3, Pallas kernels: none -> 28.5 us  [the longest x2 18 us: attention(): pl.pallas_call(functools.partial(attention_kernel, weigh), grid_spec=pltp...]
    all_gather x0 -> x1, waiting for transfers between devices: none -> 17.5 us  [body(): lax.all_gather(jnp.concatenate([k2, v2], axis=1), 'seq', axis=0, tiled=True)]
    psum x2 -> x1, blocking collectives: 26.1 us -> 42.8 us  [body(): head_total = lax.psum(partial_value.reshape(-1), ('seq', 'head'))]
    gather x8 -> x0, local copies, waits for them, and re-layouts: 12.9 us -> none  [the longest x3 5.5 us: pick_rows(): jnp.take(table, source, axis=0)]
    ppermute x4 -> x2, starting transfers between devices: 11.3 us -> 0.64 us  [the longest x1 0.56 us: body(): got_rows = lax.ppermute(sent_rows, 'seq', swap)]
    unnamed x1 -> x0, blocking collectives: 9.49 us -> none
  transfers between devices with their start and end apart: 6 -> 4, of which waited for: 0 -> 2; matrix products, arithmetic and copies ran while one was open for 33% -> 7% of each run, Pallas kernels for 0% -> 9%
where the time goes in v1:
time: 132 us
  blocking collectives  53.5 us (41%)
  Pallas kernels  28.5 us (22%)
  waiting for transfers between devices  18.7 us (14%)
  between operations  15.5 us (12%)
  local copies, waits for them, and re-layouts  7.11 us (5%)
  other arithmetic  6.05 us (5%)
  matrix products  1.52 us (1%)
    psum x1, blocking collectives, body(): head_total = lax.psum(partial_value.reshape(-1), ('seq', 'head'))  42.8 us
    pallas_call x2, Pallas kernels, attention(): pl.pallas_call(functools.partial(attention_kernel, weigh), grid_spec=pltp...  18 us
    all_gather x1, waiting for transfers between devices, body(): lax.all_gather(jnp.concatenate([k2, v2], axis=1), 'seq', axis=0, tiled=True)  17.5 us
    all_gather x1, blocking collectives, body(): pairs3 = lax.all_gather(pair3, 'seq', axis=0, tiled=True)  10.8 us
    pallas_call x1, Pallas kernels, project(): pl.pallas_call(project_kernel, grid=(depth // step,), in_specs=[pl.BlockS...  10.5 us
    unnamed x18, local copies, waits for them, and re-layouts  4.33 us
  transfers between devices with their start and end apart: 4, of which 2 were waited for; matrix products, arithmetic and copies ran while one was open for 7% of the time, Pallas kernels for 9%

profile of v1, /device:TPU:0, one launch (start us, length us, event | category | flops | bytes accessed | tf_op | source)
XLA Modules:
  0.0 131.7 jit_solution(5100435689662361876)
XLA Ops:
  7.2 0.0 copy-start
  7.2 0.0 all-gather.3.cloned.1.call-start
  7.2 1.6 %pad_maximum_fusion = bf16[256,256]{1,0:T(8,128)(2,1)} fusion(bf16[256,128]{1,0:T(8,128)(2,1)} %param.15, bf16[256,128]{1,0:T(8,128)(2,1)} %param.14), kind=kLoop, calls=%fused_computation.6 | loop fusion | flops 262144 | bytes 262144 | tf_op jit(solution)/shard_map/concatenate | solution.py:248
  8.8 0.0 all-gather.3.cloned.1.call-update
  8.9 0.0 all-gather.5.cloned.1.call-start
  8.9 1.3 fusion.8
  11.5 1.3 and_or_fusion
  12.9 1.3 add_add_fusion
  14.2 0.2 select_reduce_fusion.1
  14.4 0.0 copy-done
  14.4 0.0 copy-start.5
  14.4 0.0 copy-start.7
  14.4 0.0 copy-start.8
  14.4 0.0 copy-start.6
  14.4 0.3 convolution_convert_fusion.1
  14.8 0.6 collective-permute-start
  15.3 0.1 collective-permute-start.1
  15.4 0.2 select_reduce_fusion
  15.6 1.2 collective-permute-done.1
  16.8 0.1 fusion.4
  16.8 0.0 collective-permute-done
  16.9 1.2 select_add_fusion
  18.0 0.0 all-gather.5.cloned.1.call-update
  18.1 0.0 copy-done.5
  18.1 0.0 copy-done.7
  18.1 0.0 copy-done.8
  18.1 0.0 copy-done.6
  18.1 0.2 compare_reduce_fusion
  18.3 0.2 copy.17.rest_0_
  18.5 0.3 fusion.2
  18.8 0.1 pad_maximum_fusion.1.cos_ref
  18.9 0.1 pad_maximum_fusion.2.sin_ref
  19.0 17.5 %all-gather.3.cloned.1.call-done = bf16[2048,256]{1,0:T(8,128)(2,1)} async-done(((bf16[256,256]{1,0:T(8,128)(2,1)}), bf16[2048,256]{1,0:T(8,128)(2,1)}) %all-gather.3.cloned.1.call-update) | async-done | bytes 1048592 | tf_op jit(solution)/shard_map/all_gather | solution.py:248
  36.6 1.3 fusion.6
  37.9 0.0 copy-start.4
  37.9 1.0 copy-done.4
  38.9 0.0 copy-start.2
  38.9 11.9 %shard_map.148 = (bf16[256,1024]{1,0:T(8,128)(2,1)}, f32[1,2048]{1,0:T(1,128)S(1)}) custom-call(s32[1]{0:T(128)} %bitcast.start_ref, bf16[256,1024]{1,0:T(8,128)(2,1)S(1)} %copy-done.4, bf16[2048,128]{1,0:T(8,128)(2,1)S(1)} %get-tuple-element.12.k_ref, bf16[2048,128]{1,0:T(8,128)(2,1)S(1)} %get-tuple-element.11.v_ref, f32[256,1]{1,0:T(8,128)S(1)} %copy.17.rest_0_), custom_call_target="tpu_custom_call" | custom-call | flops 2147483648 | bytes 1048576 | tf_op jit(solution)/shard_map/pallas_call | solution.py:111
  50.8 42.8 %psum.7 = f32[2048]{0:T(1024)S(1)} all-reduce(f32[2048]{0:T(1024)S(1)} %bitcast.8), channel_id=1, replica_groups=mesh['seq'=8,'head'=4] {'seq','head'}, use_global_device_ids=true, to_apply=%region_1.2 | all-reduce | flops 2048 | bytes 16384 | tf_op jit(solution)/shard_map/psum | solution.py:252
  93.6 0.6 dynamic-slice_multiply_fusion
  94.2 0.0 all-gather.5.cloned.1.call-done.x_ref
  94.2 0.0 copy-done.2
  94.2 0.0 copy-start.1
  94.2 1.7 %copy-done.1 = bf16[144,8192]{1,0:T(8,128)(2,1)S(1)} copy-done((bf16[144,8192]{1,0:T(8,128)(2,1)S(1)}, bf16[144,8192]{1,0:T(8,128)(2,1)}, u32[]{:S(2)}) %copy-start.1) | copy-done | bytes 2359320
  95.9 0.0 copy-start.3
  95.9 1.6 %copy-done.3 = bf16[8192,128]{1,0:T(8,128)(2,1)S(1)} copy-done((bf16[8192,128]{1,0:T(8,128)(2,1)S(1)}, bf16[8192,128]{1,0:T(8,128)(2,1)}, u32[]{:S(2)}) %copy-start.3) | copy-done | bytes 2097176
  97.5 10.5 %shard_map.149 = (bf16[144,1024]{1,0:T(8,128)(2,1)S(1)}, bf16[144,256]{1,0:T(8,128)(2,1)S(1)}) custom-call(bf16[144,8192]{1,0:T(8,128)(2,1)S(1)} %copy-done.1, bf16[8192,1024]{1,0:T(8,128)(2,1)} %wq_ref.1, bf16[8192,128]{1,0:T(8,128)(2,1)S(1)} %copy-done.2, bf16[8192,128]{1,0:T(8,128)(2,1)S(1)} %copy-done.3, f32[1,1280]{1,0:T(1,128)S(1)} %broadcast_in_dim.61.bias_ref, ...), custom_call_target="tpu_custom_call" | custom-call | flops 3019898880 | bytes 20971520 | tf_op jit(solution)/shard_map/pallas_call | solution.py:163
  108.0 10.8 %all_gather.11 = bf16[1152,256]{1,0:T(8,128)(2,1)S(1)} all-gather(bf16[144,256]{1,0:T(8,128)(2,1)S(1)} %get-tuple-element.10), channel_id=1, replica_groups=mesh['seq'=8,'head'=4] {'seq'}, dimensions={0}, use_global_device_ids=true | all-gather | bytes 663552 | tf_op jit(solution)/shard_map/all_gather | solution.py:265
  118.8 6.1 %shard_map.150 = bf16[144,1024]{1,0:T(8,128)(2,1)} custom-call(s32[1]{0:T(128)} %bitcast.3.start_ref, bf16[144,1024]{1,0:T(8,128)(2,1)S(1)} %get-tuple-element.9.q_ref, bf16[1152,128]{1,0:T(8,128)(2,1)S(1)} %get-tuple-element.14.k_ref, bf16[1152,128]{1,0:T(8,128)(2,1)S(1)} %get-tuple-element.13.v_ref), custom_call_target="tpu_custom_call" | custom-call | flops 679477248 | bytes 589824 | tf_op jit(solution)/shard_map/pallas_call | solution.py:111
  (9 shorter events, 0.1 us)
Async XLA Ops:
  7.2 7.2 %copy-start = (bf16[256,2048]{1,0:T(8,128)(2,1)S(1)}, bf16[256,2048]{1,0:T(8,128)(2,1)}, u32[]{:S(2)}) copy-start(bf16[256,2048]{1,0:T(8,128)(2,1)} %param.16) | copy-start | bytes 3145732
  7.2 29.4 %all-gather.3.cloned.1.call-start = ((), (), s32[]{:S(2)}) async-start(), calls=%async_computation | async-start | bytes 1179648 | tf_op jit(solution)/shard_map/all_gather | solution.py:248
  8.9 85.3 %all-gather.5.cloned.1.call-start = ((), (), s32[]{:S(2)}) async-start(), calls=%async_computation.1 | async-start | bytes 2949120 | tf_op jit(solution)/shard_map/all_gather | solution.py:246
  14.4 3.7 %copy-start.5 = (f32[1024]{0:T(1024)S(1)}, f32[1024]{0:T(1024)}, u32[]{:S(2)}) copy-start(f32[1024]{0:T(1024)} %param.18) | copy-start | bytes 12292
  14.4 3.7 %copy-start.7 = (f32[128]{0:T(128)S(1)}, f32[128]{0:T(128)}, u32[]{:S(2)}) copy-start(f32[128]{0:T(128)} %param.22) | copy-start | bytes 1540
  14.4 3.7 %copy-start.8 = (f32[128]{0:T(128)S(1)}, f32[128]{0:T(128)}, u32[]{:S(2)}) copy-start(f32[128]{0:T(128)} %param.20) | copy-start | bytes 1540
  14.4 3.7 %copy-start.6 = (s32[256]{0:T(256)S(1)}, s32[256]{0:T(256)}, u32[]{:S(2)}) copy-start(s32[256]{0:T(256)} %param.25) | copy-start | bytes 3076
  14.8 2.1 %collective-permute-start = (bf16[112,2048]{1,0:T(8,128)(2,1)S(1)}, bf16[112,2048]{1,0:T(8,128)(2,1)S(1)}, u32[]{:S(2)}, u32[]{:S(2)}) collective-permute-start(bf16[112,2048]{1,0:T(8,128)(2,1)S(1)} %convolution_convert_fusion.1), channel_id=1, source_target_pairs={{0,4},{4,0},{8,12},{12,8},{16,20},{20,16},{24,28},{28,24},{1,5},{5... | collective-permute-start | bytes 1376264 | tf_op jit(solution)/shard_map/ppermute | solution.py:233
  15.3 1.4 %collective-permute-start.1 = (s32[112]{0:T(128)S(1)}, s32[112]{0:T(128)S(1)}, u32[]{:S(2)}, u32[]{:S(2)}) collective-permute-start(s32[112]{0:T(128)S(1)} %get-tuple-element.20), channel_id=1, source_target_pairs={{0,4},{4,0},{8,12},{12,8},{16,20},{20,16},{24,28},{28,24},{1,5},{5... | collective-permute-start | bytes 1352 | tf_op jit(solution)/shard_map/ppermute | solution.py:234
  37.9 1.0 copy-start.4
  38.9 55.3 %copy-start.2 = (bf16[8192,128]{1,0:T(8,128)(2,1)S(1)}, bf16[8192,128]{1,0:T(8,128)(2,1)}, u32[]{:S(2)}) copy-start(bf16[8192,128]{1,0:T(8,128)(2,1)} %wk_ref.1) | copy-start | bytes 6291460
  94.2 1.7 %copy-start.1 = (bf16[144,8192]{1,0:T(8,128)(2,1)S(1)}, bf16[144,8192]{1,0:T(8,128)(2,1)}, u32[]{:S(2)}) copy-start(bf16[144,8192]{1,0:T(8,128)(2,1)} %all-gather.5.cloned.1.call-done.x_ref) | copy-start | bytes 7077892
  95.9 1.6 %copy-start.3 = (bf16[8192,128]{1,0:T(8,128)(2,1)S(1)}, bf16[8192,128]{1,0:T(8,128)(2,1)}, u32[]{:S(2)}) copy-start(bf16[8192,128]{1,0:T(8,128)(2,1)} %wv_ref.1) | copy-start | bytes 6291460
Sparse Core Ops, SparseCore 0:
  10.4 26.0 all-gather.2
  38.1 51.0 all-gather.4

commit v2 on v1

--- a/solution.py
+++ b/solution.py
@@ -22,7 +22,7 @@
 
 
 def loop(count, step, carry):
-    if count <= 4:
+    if count <= 8:
         for turn in range(count):
             carry = step(turn, carry)
         return carry
@@ -125,70 +125,213 @@
     )(start.reshape(1), *operands)
 
 
-def project_kernel(
-    x_ref, wq_ref, wk_ref, wv_ref, bias_ref, cos_ref, sin_ref, q_ref, kv_ref, acc_q, acc_k, acc_v
+MESH = pl.DeviceIdType.MESH
+
+
+def fused_kernel(
+    seq_count, head_count,
+    q_ref, kv_ref, text_ref, x_ref, bias_ref, cos_ref, sin_ref, wq_ref, wk_ref, wv_ref,
+    attn_ref, imp_ref, q3_ref, kv3_ref,
+    kv_all, x_all, score, parts, part_all, mine, mine_all, wq, wk, wv, acc_q, acc_k, acc_v,
+    kv_send, kv_recv, x_send, x_recv, p_send, p_recv, m_send, m_recv, w_sem,
 ):
-    @pl.when(pl.program_id(0) == 0)
-    def _():
-        columns = acc_q.shape[1]
-        acc_q[...] = jnp.broadcast_to(bias_ref[:, :columns], acc_q.shape)
-        acc_k[...] = jnp.broadcast_to(bias_ref[:, columns : columns + HD], acc_k.shape)
-        acc_v[...] = jnp.broadcast_to(bias_ref[:, columns + HD :], acc_v.shape)
-
+    seq, head = lax.axis_index("seq"), lax.axis_index("head")
+    rows = q_ref.shape[0]
+    depth = x_ref.shape[1]
+    columns = q_ref.shape[1]
+    scale = 1.0 / math.sqrt(HD)
+
+    def weights_in(turn):
+        owner = lax.rem(head + turn, head_count)
+        span = pl.ds(pl.multiple_of(owner * depth, 128), depth)
+        pairs = ((wq_ref, wq), (wk_ref, wk), (wv_ref, wv))
+        return [pltpu.make_async_copy(f.at[span, :], t.at[turn], w_sem.at[turn, i]) for i, (f, t) in enumerate(pairs)]
+
+    for turn in range(head_count):
+        for copy in weights_in(turn):
+            copy.start()
+
+    def seq_peer(k):
+        return lax.rem(seq + k, seq_count)
+
+    def head_peer(k):
+        return lax.rem(head + k, head_count)
+
+    barrier = pltpu.get_barrier_semaphore()
+    for k in range(1, seq_count):
+        pl.semaphore_signal(barrier, inc=1, device_id=(seq_peer(k), head), device_id_type=MESH)
+    for k in range(1, head_count):
+        pl.semaphore_signal(barrier, inc=1, device_id=(seq, head_peer(k)), device_id_type=MESH)
+    pl.semaphore_wait(barrier, seq_count + head_count - 2)
+
+    def kv_copy(k):
+        return pltpu.make_async_remote_copy(
+            src_ref=kv_ref, dst_ref=kv_all.at[seq_count - k], send_sem=kv_send.at[k],
+            recv_sem=kv_recv.at[seq_count - k], device_id=(seq_peer(k), head), device_id_type=MESH,
+        )
+
+    def x_copy(k):
+        return pltpu.make_async_remote_copy(
+            src_ref=x_ref, dst_ref=x_all.at[head_count - k], send_sem=x_send.at[k],
+            recv_sem=x_recv.at[head_count - k], device_id=(seq, head_peer(k)), device_id_type=MESH,
+        )
+
+    def part_copy(k):
+        return pltpu.make_async_remote_copy(
+            src_ref=parts.at[k], dst_ref=part_all.at[seq_count - k], send_sem=p_send.at[k],
+            recv_sem=p_recv.at[seq_count - k], device_id=(seq_peer(k), head), device_id_type=MESH,
+        )
+
+    def mine_copy(k):
+        return pltpu.make_async_remote_copy(
+            src_ref=mine, dst_ref=mine_all.at[head_count - k], send_sem=m_send.at[k],
+            recv_sem=m_recv.at[head_count - k], device_id=(seq, head_peer(k)), device_id_type=MESH,
+        )
+
+    for k in range(1, seq_count):
+        kv_copy(k).start()
+    for k in range(1, head_count):
+        x_copy(k).start()
+    kv_all[0] = kv_ref[...]
+    parts[...] = jnp.zeros_like(parts)
+
+    for copy in weights_in(0):
+        copy.wait()
     x = x_ref[...]
-    acc_q[...] += jnp.dot(x, wq_ref[...], preferred_element_type=jnp.float32)
-    acc_k[...] += jnp.dot(x, wk_ref[...], preferred_element_type=jnp.float32)
-    acc_v[...] += jnp.dot(x, wv_ref[...], preferred_element_type=jnp.float32)
-
-    @pl.when(pl.program_id(0) == pl.num_programs(0) - 1)
-    def _():
-        cosine, sine = cos_ref[...], sin_ref[...]
-
-        def turned(u):
-            return (u * cosine + pltpu.roll(u, HD // 2, 1) * sine).astype(jnp.bfloat16)
-
-        for head in range(acc_q.shape[1] // HD):
-            part = slice(head * HD, (head + 1) * HD)
-            q_ref[:, part] = turned(acc_q[:, part])
-        kv_ref[:, :HD] = turned(acc_k[...])
-        kv_ref[:, HD:] = acc_v[...].astype(jnp.bfloat16)
-
-
-def project(x, cosine, sine, w_query, w_key, w_value, bias):
-    rows, depth = x.shape
-    columns = w_query.shape[1]
-    step = 1024
-    whole = lambda shape: pl.BlockSpec(shape, lambda i: (0, 0))
-    down = lambda width: pl.BlockSpec((step, width), lambda i: (i, 0))
+    acc_q[...] = bias_ref[:, :columns] + jnp.dot(x, wq[0], preferred_element_type=jnp.float32)
+    acc_k[...] = bias_ref[:, columns : columns + HD] + jnp.dot(x, wk[0], preferred_element_type=jnp.float32)
+    acc_v[...] = bias_ref[:, columns + HD :] + jnp.dot(x, wv[0], preferred_element_type=jnp.float32)
+    for k in range(1, seq_count):
+        kv_copy(k).wait_recv()
+
+    row = seq * rows + lax.broadcasted_iota(jnp.int32, (rows, rows), 0)
+    ahead = row - lax.broadcasted_iota(jnp.int32, (rows, rows), 1)
+
+    def one_head(h, state):
+        span = pl.ds(pl.multiple_of(h * HD, 128), HD)
+        queries = q_ref[:, span]
+
+        def first(k, top):
+            scores = lax.dot_general(
+                queries, kv_all[k, :, :HD], (((1,), (1,)), ((), ())), preferred_element_type=jnp.float32
+            )
+            scores = jnp.where(ahead >= seq_peer(k) * rows, scores, -1e30)
+            score[k] = scores
+            for part in range(rows // 128):
+                top = jnp.maximum(top, scores[:, part * 128 : (part + 1) * 128])
+            return top
+
+        top = loop(seq_count, first, jnp.full((rows, 128), -1e30, jnp.float32))
+        top = jnp.max(top, axis=1, keepdims=True)
+
+        def second(k, carry):
+            total, summed = carry
+            weights = jnp.exp((score[k] - top) * scale)
+            score[k] = weights
+            for part in range(rows // 128):
+                total = total + weights[:, part * 128 : (part + 1) * 128]
+            summed = summed + jnp.dot(
+                weights.astype(jnp.bfloat16), kv_all[k, :, HD:], preferred_element_type=jnp.float32
+            )
+            return (total, summed)
+
+        blank = jnp.zeros((rows, 128), jnp.float32)
+        total, summed = loop(seq_count, second, (blank, blank))
+        inverse = 1.0 / jnp.sum(total, axis=1, keepdims=True)
+        attn_ref[:, span] = (summed * inverse).astype(jnp.bfloat16)
+        share = inverse * text_ref[...]
+
+        def third(k, carry):
+            parts[k] += jnp.sum((score[k] * share).reshape(rows // 8, 8, rows), axis=0)
+            return carry
+
+        loop(seq_count, third, 0)
+        return state
+
+    lax.fori_loop(0, columns // HD, one_head, 0)
+    for turn in range(1, head_count):
+        for copy in weights_in(turn):
+            copy.wait()
+        x_copy(head_count - turn).wait_recv()
+        x = x_all[turn]
+        acc_q[...] += jnp.dot(x, wq[turn], preferred_element_type=jnp.float32)
+        acc_k[...] += jnp.dot(x, wk[turn], preferred_element_type=jnp.float32)
+        acc_v[...] += jnp.dot(x, wv[turn], preferred_element_type=jnp.float32)
+        if turn == 1:
+            for k in range(1, seq_count):
+                part_copy(k).start()
+        if turn == head_count - 1:
+            gathered = parts[0]
+            for k in range(1, seq_count):
+                part_copy(k).wait_recv()
+            for k in range(1, seq_count):
+                gathered = gathered + part_all[k]
+            mine[...] = gathered
+
+    cosine, sine = cos_ref[...], sin_ref[...]
+
+    def turned(u):
+        return (u * cosine + pltpu.roll(u, HD // 2, 1) * sine).astype(jnp.bfloat16)
+
+    for h in range(columns // HD):
+        part = slice(h * HD, (h + 1) * HD)
+        q3_ref[:, part] = turned(acc_q[:, part])
+    kv3_ref[:, :HD] = turned(acc_k[...])
+    kv3_ref[:, HD:] = acc_v[...].astype(jnp.bfloat16)
+    for k in range(1, head_count):
+        mine_copy(k).start()
+    everyone = mine[...]
+    for k in range(1, head_count):
+        mine_copy(k).wait_recv()
+    for k in range(1, head_count):
+        everyone = everyone + mine_all[k]
+    imp_ref[...] = everyone
+    for k in range(1, seq_count):
+        kv_copy(k).wait_send()
+        part_copy(k).wait_send()
+    for k in range(1, head_count):
+        x_copy(k).wait_send()
+        mine_copy(k).wait_send()
+
+
+def fused(seq_count, head_count, q2, kv2, text, x, bias, cosine, sine, w_query, w_key, w_value):
+    rows, columns = q2.shape
+    kept, depth = x.shape
+    vmem = pl.BlockSpec(memory_space=pltpu.VMEM)
+    hbm = pl.BlockSpec(memory_space=pl.ANY)
+    dma = pltpu.SemaphoreType.DMA
     return pl.pallas_call(
-        project_kernel,
-        grid=(depth // step,),
-        in_specs=[
-            pl.BlockSpec((rows, step), lambda i: (0, i)),
-            down(columns),
-            down(HD),
-            down(HD),
-            whole((1, columns + 2 * HD)),
-            whole((rows, HD)),
-            whole((rows, HD)),
-        ],
-        out_specs=[whole((rows, columns)), whole((rows, 2 * HD))],
+        functools.partial(fused_kernel, seq_count, head_count),
+        in_specs=[vmem] * 7 + [hbm] * 3,
+        out_specs=[vmem] * 4,
         out_shape=[
             jax.ShapeDtypeStruct((rows, columns), jnp.bfloat16),
-            jax.ShapeDtypeStruct((rows, 2 * HD), jnp.bfloat16),
+            jax.ShapeDtypeStruct((8, rows), jnp.float32),
+            jax.ShapeDtypeStruct((kept, columns), jnp.bfloat16),
+            jax.ShapeDtypeStruct((kept, 2 * HD), jnp.bfloat16),
         ],
         scratch_shapes=[
-            pltpu.VMEM((rows, columns), jnp.float32),
-            pltpu.VMEM((rows, HD), jnp.float32),
-            pltpu.VMEM((rows, HD), jnp.float32),
+            pltpu.VMEM((seq_count, rows, 2 * HD), jnp.bfloat16),
+            pltpu.VMEM((head_count, kept, depth), jnp.bfloat16),
+            pltpu.VMEM((seq_count, rows, rows), jnp.float32),
+            pltpu.VMEM((seq_count, 8, rows), jnp.float32),
+            pltpu.VMEM((seq_count, 8, rows), jnp.float32),
+            pltpu.VMEM((8, rows), jnp.float32),
+            pltpu.VMEM((head_count, 8, rows), jnp.float32),
+            pltpu.VMEM((head_count, depth, columns), jnp.bfloat16),
+            pltpu.VMEM((head_count, depth, HD), jnp.bfloat16),
+            pltpu.VMEM((head_count, depth, HD), jnp.bfloat16),
+            pltpu.VMEM((kept, columns), jnp.float32),
+            pltpu.VMEM((kept, HD), jnp.float32),
+            pltpu.VMEM((kept, HD), jnp.float32),
+            dma((seq_count,)), dma((seq_count,)), dma((head_count,)), dma((head_count,)),
+            dma((seq_count,)), dma((seq_count,)), dma((head_count,)), dma((head_count,)),
+            dma((head_count, 3)),
         ],
-        compiler_params=pltpu.CompilerParams(vmem_limit_bytes=32 * 1024 * 1024),
-        cost_estimate=pl.CostEstimate(
-            flops=2 * rows * depth * (columns + 2 * HD),
-            bytes_accessed=2 * depth * (columns + 2 * HD),
-            transcendentals=0,
+        compiler_params=pltpu.CompilerParams(
+            collective_id=0, has_side_effects=True, vmem_limit_bytes=58 * 1024 * 1024
         ),
-    )(x, w_query, w_key, w_value, bias, cosine, sine)
+    )(q2, kv2, text, x, bias, cosine, sine, w_query, w_key, w_value)
 
 
 def body(
@@ -243,17 +386,8 @@
 
     kept_rows = own_rows + landed(got_rows)
     kept_pos = own_pos + landed(got_pos)
-    full_rows = lax.all_gather(kept_rows, "head", axis=1, tiled=True)
-
-    pairs = lax.all_gather(jnp.concatenate([k2, v2], axis=1), "seq", axis=0, tiled=True)
     query_pos = first_row + jnp.arange(rows, dtype=jnp.int32)
     is_text = jnp.any(query_pos[:, None] == text_rows[None, :], axis=1, keepdims=True).astype(jnp.float32)
-    attn2, partial_value = attention(first_row, q2, pairs[:, :HD], pairs[:, HD:], is_text)
-    head_total = lax.psum(partial_value.reshape(-1), ("seq", "head"))
-    importance = lax.dynamic_slice_in_dim(head_total, first_row, rows, 0) * (
-        rows * seq_count / (GROUP * head_count * text)
-    )
-
     half = HD // 2
     freqs = THETA ** (-(jnp.arange(half, dtype=jnp.float32) * 2.0) / HD)
     angles = kept_pos.astype(jnp.float32)[:, None] * freqs[None, :]
@@ -261,7 +395,11 @@
     cosine = jnp.concatenate([cosine, cosine], axis=1)
     sine = jnp.concatenate([-sine, sine], axis=1)
     bias = jnp.concatenate([b_query, b_key, b_value])[None, :]
-    queries3, pair3 = project(full_rows, cosine, sine, w_query, w_key, w_value, bias)
+    attn2, shares, queries3, pair3 = fused(
+        seq_count, head_count, q2, jnp.concatenate([k2, v2], axis=1), is_text, kept_rows, bias, cosine, sine,
+        w_query, w_key, w_value,
+    )
+    importance = jnp.sum(shares, axis=0) * (rows * seq_count / (GROUP * head_count * text))
     pairs3 = lax.all_gather(pair3, "seq", axis=0, tiled=True)
     (attn3,) = attention(seq_rank * per_device, queries3, pairs3[:, :HD], pairs3[:, HD:])
     return (attn2, importance, attn3)

time: 132 us -> 98.7 us (0.75)
  Pallas kernels: 28.5 us -> 73.7 us
  blocking collectives: 53.5 us -> 9.71 us
  waiting for transfers between devices: 18.7 us -> 0.01 us
  between operations: 15.5 us -> 2.15 us
  local copies, waits for them, and re-layouts: 7.11 us -> 3.6 us
    pallas_call x1, Pallas kernels: 10.5 us -> 67.6 us  [fused(): pl.pallas_call(functools.partial(fused_kernel, seq_count, head_count), in...]
    psum x1 -> x0, blocking collectives: 42.8 us -> none  [body(): head_total = lax.psum(partial_value.reshape(-1), ('seq', 'head'))]
    all_gather x2 -> x0, waiting for transfers between devices: 17.6 us -> none  [the longest x1 17.5 us: body(): lax.all_gather(jnp.concatenate([k2, v2], axis=1), 'seq', axis=0, tiled=True)]
    pallas_call x2 -> x1, Pallas kernels: 18 us -> 6.08 us  [attention(): pl.pallas_call(functools.partial(attention_kernel, weigh), grid_spec=pltp...]
    unnamed x18 -> x19, local copies, waits for them, and re-layouts: 4.33 us -> 0.84 us
  transfers between devices with their start and end apart: 4 -> 2, of which waited for: 2 -> 0; matrix products, arithmetic and copies ran while one was open for 7% -> 5% of each run, Pallas kernels for 9% -> 0%
where the time goes in v2:
time: 98.7 us; the launch traced here: 98.3 us
  Pallas kernels  73.7 us (75%)
  blocking collectives  9.71 us (10%)
  other arithmetic  7.06 us (7%)
  local copies, waits for them, and re-layouts  3.6 us (4%)
  between operations  2.15 us (2%)
  matrix products  1.53 us (2%)
    pallas_call x1, Pallas kernels, fused(): pl.pallas_call(functools.partial(fused_kernel, seq_count, head_count), in...  67.6 us
    all_gather x1, blocking collectives, body(): pairs3 = lax.all_gather(pair3, 'seq', axis=0, tiled=True)  9.71 us
    pallas_call x1, Pallas kernels, attention(): pl.pallas_call(functools.partial(attention_kernel, weigh), grid_spec=pltp...  6.08 us
  transfers between devices with their start and end apart: 2, of which 0 were waited for; matrix products, arithmetic and copies ran while one was open for 5% of the time, Pallas kernels for 0%

profile of v2, /device:TPU:0, one launch (start us, length us, event | category | flops | bytes accessed | tf_op | source)
XLA Modules:
  0.0 98.3 jit_solution(6426222298488872828)
XLA Ops:
  0.6 0.0 copy-start
  0.6 0.0 copy-start.6
  0.7 0.0 copy-start.3
  0.7 0.0 copy-start.4
  0.7 0.0 copy-start.7
  0.7 0.0 copy-start.8
  0.7 0.0 copy-start.5
  0.7 1.3 %fusion.7 = (s32[1]{0:T(128)}, s32[1]{0:T(128)}) fusion(s32[2]{0:T(128)} %param.24), kind=kLoop, calls=%fused_computation.39 | loop fusion | bytes 16 | tf_op jit(solution)/shard_map/slice | solution.py:352
  3.4 1.3 %and_or_fusion = pred[256]{0:T(512)(128)(4,1)S(1)} fusion(s32[]{:T(128)} %bitcast.2, s32[]{:T(128)} %bitcast.1), kind=kLoop, calls=%fused_computation.19 | loop fusion | flops 4864 | bytes 264 | tf_op jit(solution)/shard_map/or | solution.py:362
  4.7 1.3 %add_add_fusion = (s32[256]{0:T(256)S(1)}, s32[256]{0:T(256)S(1)}) fusion(s32[256]{0:T(256)} %param.23, s32[]{:T(128)} %bitcast.1, s32[]{:T(128)S(6)} %select_n.99), kind=kLoop, calls=%fused_computation.26 | loop fusion | flops 4864 | bytes 3080 | tf_op jit(solution)/shard_map/add | solution.py:368
  6.0 0.2 select_reduce_fusion.1
  6.2 0.6 collective-permute-start.1
  6.8 0.0 copy-done
  6.8 0.3 convolution_convert_fusion.1
  7.1 0.1 collective-permute-start
  7.2 0.2 select_reduce_fusion
  7.4 0.0 copy-done.6
  7.4 0.2 compare_reduce_fusion
  7.6 0.0 copy-done.3
  7.6 0.0 copy-done.4
  7.6 0.7 pad_maximum_fusion.kv_ref
  8.3 0.0 copy-done.7
  8.3 0.0 copy-done.8
  8.3 0.0 copy-done.5
  8.4 0.6 broadcast_in_dim.61.bias_ref
  8.9 0.8 copy.17.text_ref
  9.7 0.0 collective-permute-done.1
  9.7 0.1 fusion.4
  9.8 0.3 fusion.2
  10.2 0.7 pad_maximum_fusion.1.cos_ref
  10.9 0.7 pad_maximum_fusion.2.sin_ref
  11.6 0.0 collective-permute-done
  11.6 1.2 %select_add_fusion.x_ref = bf16[144,2048]{1,0:T(8,128)(2,1)} fusion(bf16[112,2048]{1,0:T(8,128)(2,1)S(1)} %collective-permute-done, pred[]{:T(512)S(6)} %eq.103, bf16[256,2048]{1,0:T(8,128)(2,1)S(1)} %copy-done, s32[144]{0:T(256)S(1)} %get-tuple-element.17), kind=kOutput, calls=%fused_computation.2 | convolution fusion | flops 152801280 | bytes 2097729 | tf_op jit(solution)/shard_map/dot_general | solution.py:370
  12.8 67.6 %shard_map.148 = (bf16[256,1024]{1,0:T(8,128)(2,1)}, f32[8,256]{1,0:T(8,128)}, bf16[144,1024]{1,0:T(8,128)(2,1)}, bf16[144,256]{1,0:T(8,128)(2,1)}) custom-call(bf16[256,1024]{1,0:T(8,128)(2,1)} %q_ref.1, bf16[256,256]{1,0:T(8,128)(2,1)} %pad_maximum_fusion.kv_ref, f32[256,1]{1,0:T(8,128)} %copy.17.text_ref, bf16[144,2048]{1,0:T(8,128)(2,1)} %select_add_fusion.x_ref, ...), custom_call_target="tpu_custom_call" | custom-call | tf_op jit(solution)/shard_map/pallas_call | solution.py:303
  80.4 0.0 copy-start.1
  80.4 0.8 reduce_sum.29
  81.1 0.6 broadcast_multiply_fusion
  81.7 9.7 %all_gather.3 = bf16[1152,256]{1,0:T(8,128)(2,1)S(1)} all-gather(bf16[144,256]{1,0:T(8,128)(2,1)} %get-tuple-element.10), channel_id=1, replica_groups=mesh['seq'=8,'head'=4] {'seq'}, dimensions={0}, use_global_device_ids=true | all-gather | bytes 663552 | tf_op jit(solution)/shard_map/all_gather | solution.py:403
  91.5 0.0 copy-done.1
  91.5 0.0 copy-start.2
  91.5 6.1 %shard_map.149 = bf16[144,1024]{1,0:T(8,128)(2,1)} custom-call(s32[1]{0:T(128)} %bitcast.3.start_ref, bf16[144,1024]{1,0:T(8,128)(2,1)S(1)} %copy-done.1, bf16[1152,128]{1,0:T(8,128)(2,1)S(1)} %get-tuple-element.12.k_ref, bf16[1152,128]{1,0:T(8,128)(2,1)S(1)} %get-tuple-element.11.v_ref), custom_call_target="tpu_custom_call" | custom-call | flops 679477248 | bytes 589824 | tf_op jit(solution)/shard_map/pallas_call | solution.py:111
  97.6 0.0 copy-done.2
  97.6 0.8 copy.19
  (8 shorter events, 0.1 us)
Async XLA Ops:
  0.6 6.2 %copy-start = (bf16[256,2048]{1,0:T(8,128)(2,1)S(1)}, bf16[256,2048]{1,0:T(8,128)(2,1)}, u32[]{:S(2)}) copy-start(bf16[256,2048]{1,0:T(8,128)(2,1)} %param.16) | copy-start | bytes 3145732
  0.6 6.8 %copy-start.6 = (s32[256]{0:T(256)S(1)}, s32[256]{0:T(256)}, u32[]{:S(2)}) copy-start(s32[256]{0:T(256)} %param.25) | copy-start | bytes 3076
  0.7 7.0 %copy-start.3 = (bf16[256,128]{1,0:T(8,128)(2,1)S(1)}, bf16[256,128]{1,0:T(8,128)(2,1)}, u32[]{:S(2)}) copy-start(bf16[256,128]{1,0:T(8,128)(2,1)} %param.15) | copy-start | bytes 196612
  0.7 7.0 %copy-start.4 = (bf16[256,128]{1,0:T(8,128)(2,1)S(1)}, bf16[256,128]{1,0:T(8,128)(2,1)}, u32[]{:S(2)}) copy-start(bf16[256,128]{1,0:T(8,128)(2,1)} %param.14) | copy-start | bytes 196612
  0.7 7.6 %copy-start.7 = (f32[128]{0:T(128)S(1)}, f32[128]{0:T(128)}, u32[]{:S(2)}) copy-start(f32[128]{0:T(128)} %param.22) | copy-start | bytes 1540
  0.7 7.6 %copy-start.8 = (f32[128]{0:T(128)S(1)}, f32[128]{0:T(128)}, u32[]{:S(2)}) copy-start(f32[128]{0:T(128)} %param.20) | copy-start | bytes 1540
  0.7 7.6 %copy-start.5 = (f32[1024]{0:T(1024)S(1)}, f32[1024]{0:T(1024)}, u32[]{:S(2)}) copy-start(f32[1024]{0:T(1024)} %param.18) | copy-start | bytes 12292
  6.2 3.5 %collective-permute-start.1 = (s32[112]{0:T(128)S(1)}, s32[112]{0:T(128)S(1)}, u32[]{:S(2)}, u32[]{:S(2)}) collective-permute-start(s32[112]{0:T(128)S(1)} %get-tuple-element.18), channel_id=1, source_target_pairs={{0,4},{4,0},{8,12},{12,8},{16,20},{20,16},{24,28},{28,24},{1,5},{5... | collective-permute-start | bytes 1352 | tf_op jit(solution)/shard_map/ppermute | solution.py:377
  7.1 4.5 %collective-permute-start = (bf16[112,2048]{1,0:T(8,128)(2,1)S(1)}, bf16[112,2048]{1,0:T(8,128)(2,1)S(1)}, u32[]{:S(2)}, u32[]{:S(2)}) collective-permute-start(bf16[112,2048]{1,0:T(8,128)(2,1)S(1)} %convolution_convert_fusion.1), channel_id=1, source_target_pairs={{0,4},{4,0},{8,12},{12,8},{16,20},{20,16},{24,28},{28,24},{1,5},{5... | collective-permute-start | bytes 1376264 | tf_op jit(solution)/shard_map/ppermute | solution.py:376
  80.4 11.1 %copy-start.1 = (bf16[144,1024]{1,0:T(8,128)(2,1)S(1)}, bf16[144,1024]{1,0:T(8,128)(2,1)}, u32[]{:S(2)}) copy-start(bf16[144,1024]{1,0:T(8,128)(2,1)} %get-tuple-element.9.q_ref) | copy-start | bytes 884740
  91.5 6.1 %copy-start.2 = (bf16[256,1024]{1,0:T(8,128)(2,1)S(1)}, bf16[256,1024]{1,0:T(8,128)(2,1)}, u32[]{:S(2)}) copy-start(bf16[256,1024]{1,0:T(8,128)(2,1)} %get-tuple-element.27) | copy-start | bytes 1572868
